TPU v7x, 32 devices: a whole 2x2x4 slice. The times are simulated.
32 devices in a mesh: pos: 2 (over x), gz: 16 (over z, y, core).
Axes of the slice: x: 2, y: 2, z: 4, core: 2. Of those that a mesh axis runs over, the one named last changes fastest.
Arguments:
- source: float32 [16, 512, 256], P('gz', 'pos'), parts along dimension 1
- regions: int32 [16, 512, 256], P('gz', 'pos'), parts along dimension 1, may hold values from 0 to 3
- reluctivity: float32 [4], replicated, may hold values from 0.25 to 2
- levels: float32 [4], replicated, may hold values from 0.5 to 1.5
- seeds: int32 [4, 4], replicated, may hold values from 0 to 3, as said below
- band_cells: int32 [4096], P('pos'), parts along dimension 0, may hold values from 0 to 65535, as said below
- sector_order: int32 [4096], P('pos'), parts along dimension 0, may hold values from 0 to 2047, each once
Outputs:
- solution: float32 [4, 16, 512, 256], P(None, 'gz', 'pos'), parts along dimension 2
- forces: float32 [2, 8, 32, 16], P(None, 'pos', 'gz'), parts along dimension 1
There are 2 independent parts, one for each index of `pos`. A program takes and returns all parts, laid end to end along the dimension named above; an argument that names none is the same for every part. Nothing has to cross between parts.
Inputs may be any that keep to these rules, and one draw needn't show every extreme that they name: `seeds`: every level is named by exactly 4 entries. `band_cells`: distinct cells. `sector_order`: each band entry once.
All inputs are finite; a program needn't handle non-finite values.
Results may differ from a plain program's by a relative error of at most 0.0003.
Values sent between devices are 32-bit elements; how exact they have to be, the bound alone decides.
No kernel may reach another device: no remote copies, remote signals or barrier semaphores. Data moves between devices by JAX's collectives and lax.ppermute only.
A program may use at most 128 MiB of HBM per device.

v0:
```python
import jax
import jax.numpy as jnp
from jax import lax
from jax.sharding import PartitionSpec as P

ITERS = 2
PER_SEC = 64
MASS_SHIFT = 0.5


def with_halo(block, sides, width):
    for axis, dim in sides:
        count = lax.axis_size(axis)
        forward = [(i, i + 1) for i in range(count - 1)]
        backward = [(target, source) for source, target in forward]
        low = lax.ppermute(
            lax.slice_in_dim(block, block.shape[dim] - width, None, axis=dim), axis, forward
        )
        high = lax.ppermute(lax.slice_in_dim(block, 0, width, axis=dim), axis, backward)
        block = jnp.concatenate([low, block, high], axis=dim)
    return block


def face_weights(reluct_cell, padded):
    return (
        0.5 * (reluct_cell + padded[:-2, 1:-1, 1:-1]),
        0.5 * (reluct_cell + padded[2:, 1:-1, 1:-1]),
        0.5 * (reluct_cell + padded[1:-1, :-2, 1:-1]),
        0.5 * (reluct_cell + padded[1:-1, 2:, 1:-1]),
        0.5 * (reluct_cell + padded[1:-1, 1:-1, :-2]),
        0.5 * (reluct_cell + padded[1:-1, 1:-1, 2:]),
    )


def apply_stencil(field, padded, weights):
    total = MASS_SHIFT * field
    total = total + weights[0][None] * (field - padded[:, :-2, 1:-1, 1:-1])
    total = total + weights[1][None] * (field - padded[:, 2:, 1:-1, 1:-1])
    total = total + weights[2][None] * (field - padded[:, 1:-1, :-2, 1:-1])
    total = total + weights[3][None] * (field - padded[:, 1:-1, 2:, 1:-1])
    total = total + weights[4][None] * (field - padded[:, 1:-1, 1:-1, :-2])
    total = total + weights[5][None] * (field - padded[:, 1:-1, 1:-1, 2:])
    return total


def operate(field, weights):
    axial = with_halo(field, (("gz", 1),), 1)
    padded = jnp.pad(axial, ((0, 0), (0, 0), (1, 1), (1, 1)))
    return apply_stencil(field, padded, weights)


def band_stress(field, band_cells, sector_order):
    count_cols, depth, width_x, width_y = field.shape
    padded = jnp.pad(field, ((0, 0), (0, 0), (1, 1), (1, 1)))
    flux_x = 0.5 * (padded[:, :, 1:-1, 2:] - padded[:, :, 1:-1, :-2])
    flux_y = -0.5 * (padded[:, :, 2:, 1:-1] - padded[:, :, :-2, 1:-1])
    ordered = jnp.take(band_cells, sector_order)
    picked_x = jnp.take(flux_x.reshape(count_cols, depth, width_x * width_y), ordered, axis=2)
    picked_y = jnp.take(flux_y.reshape(count_cols, depth, width_x * width_y), ordered, axis=2)
    row_index = (ordered // width_y).astype(jnp.float32)
    column_index = (ordered % width_y).astype(jnp.float32)
    normal_x = (row_index - 0.5 * (width_x - 1)) / (0.5 * width_x)
    normal_y = (column_index - 0.5 * (width_y - 1)) / (0.5 * width_y)
    normal_part = picked_x * normal_x + picked_y * normal_y
    half_square = 0.5 * (picked_x * picked_x + picked_y * picked_y)
    force_x = picked_x * normal_part - half_square * normal_x
    force_y = picked_y * normal_part - half_square * normal_y
    return jnp.stack([force_x, force_y])


def column_sum(first, second):
    return jnp.sum(first * second, axis=(1, 2, 3))


def widen(vector):
    return vector[:, None, None, None]


def squares(residual):
    return lax.psum(column_sum(residual, residual), "gz")


def body(source, regions, reluctivity, levels, seeds, band_cells, sector_order):
    count_regions = reluctivity.shape[0]
    count_levels = levels.shape[0]
    count_cols = seeds.shape[0]
    level_pick = (
        seeds[:, :, None] == jnp.arange(count_levels, dtype=jnp.int32)[None, None, :]
    ).astype(jnp.float32)
    strength = jnp.sum(level_pick * levels[None, None, :], axis=2)
    reluct_cell = jnp.zeros(source.shape, jnp.float32)
    scaling = jnp.zeros((count_cols,) + source.shape, jnp.float32)
    for region in range(count_regions):
        member = (regions == region).astype(jnp.float32)
        reluct_cell = reluct_cell + reluctivity[region] * member
        scaling = scaling + widen(strength[:, region]) * member[None]
    right_side = scaling * source[None]
    axial_reluct = with_halo(reluct_cell, (("gz", 0),), 1)
    weights = face_weights(reluct_cell, jnp.pad(axial_reluct, ((0, 0), (1, 1), (1, 1))))
    solution = jnp.zeros_like(right_side)
    residual = right_side
    direction = right_side
    norm_now = squares(residual)
    for iteration in range(ITERS):
        image = operate(direction, weights)
        curvature = lax.psum(column_sum(direction, image), "gz")
        step_size = norm_now / curvature
        solution = solution + widen(step_size) * direction
        residual = residual - widen(step_size) * image
        if iteration + 1 < ITERS:
            norm_next = squares(residual)
            direction = residual + widen(norm_next / norm_now) * direction
            norm_now = norm_next
    stress = band_stress(solution, band_cells, sector_order)
    depth = stress.shape[2]
    band_total = stress.shape[3]
    cell_forces = stress.reshape(2 * count_cols, depth, band_total // PER_SEC, PER_SEC)
    sector_sums = jnp.sum(cell_forces, axis=-1)
    gathered = lax.all_to_all(sector_sums, "gz", split_axis=2, concat_axis=1, tiled=True)
    full_depth = gathered.shape[1]
    local_sectors = gathered.shape[2]
    return (
        solution,
        gathered.reshape(2, count_cols, full_depth, local_sectors).transpose(0, 1, 3, 2),
    )


def solution(mesh):
    in_specs = (P("gz", "pos", None), P("gz", "pos", None), P(), P(), P(), P("pos"), P("pos"))
    out_specs = (P(None, "gz", "pos", None), P(None, "pos", "gz", None))
    return jax.shard_map(body, mesh=mesh, in_specs=in_specs, out_specs=out_specs, check_vma=False)
```

profile of v0, /device:TPU:0, one launch (start us, length us, event | category | flops | bytes accessed | tf_op | source)
XLA Modules:
  0.0 248.1 jit_solution(8172619403252615749)
XLA Ops:
  0.6 1.5 fusion.45
  3.2 3.7 %select_add_fusion = (f32[1,256,256]{2,1,0:T(8,128)S(1)}, pred[1,256,256]{2,1,0:T(8,128)(4,1)S(1)}, pred[1,256,256]{2,1,0:T(8,128)(4,1)S(1)}, pred[1,256,256]{2,1,0:T(8,128)(4,1)S(1)}, pred[1,256,256]{2,1,0:T(8,128)(4,1)S(1)}) fusion(f32[]{:T(128)} %bitcast.8, f32[]{:T(128)} %bitcast.7, f32[]{:T(128)} %bitcast.6, f32[]{:T(128)} %bitcast.5, ...), kind=kLoop, calls=%fused_computation.82 | loop fusion | flops 720896 | bytes 786448 | tf_op jit(solution)/shard_map/add | solution.py:95
  7.0 1.3 add_multiply_fusion
  8.3 2.4 collective-permute-start.1
  10.7 1.3 collective-permute-start.3
  12.0 5.1 %collective-permute-start = (f32[1,256,256]{2,1,0:T(8,128)S(1)}, f32[1,256,256]{2,1,0:T(8,128)S(1)}, u32[]{:S(2)}, u32[]{:S(2)}) collective-permute-start(f32[1,256,256]{2,1,0:T(8,128)S(1)} %get-tuple-element.24), channel_id=1, source_target_pairs={{0,1},{1,2},{2,3},{3,4},{4,5},{5,6},{6,7},{7,8},{8,9},{9,10},{10,1... | collective-permute-start | bytes 786440 | tf_op jit(solution)/shard_map/ppermute | solution.py:16
  17.2 1.3 collective-permute-start.2
  18.5 3.3 %collective-permute-done.2 = f32[1,256,256]{2,1,0:T(8,128)S(1)} collective-permute-done((f32[1,256,256]{2,1,0:T(8,128)S(1)}, f32[1,256,256]{2,1,0:T(8,128)S(1)}, u32[]{:S(2)}, u32[]{:S(2)}) %collective-permute-start.2) | collective-permute-done | bytes 262176 | tf_op jit(solution)/shard_map/ppermute | solution.py:19
  22.6 2.4 select_maximum_fusion.2
  25.0 1.8 multiply_reduce_fusion.1
  26.9 50.9 %all-reduce.4 = (f32[4]{0:T(128)S(1)}, f32[4]{0:T(128)S(1)}) all-reduce(f32[4]{0:T(128)S(1)} %get-tuple-element.14, f32[4]{0:T(128)S(1)} %get-tuple-element.13), channel_id=1, replica_groups=mesh['pos'=2,'gz'=16] {'gz'}, use_global_device_ids=true, to_apply=%region_2.3 | all-reduce | flops 8 | bytes 64 | tf_op jit(solution)/shard_map/psum | solution.py:80
  78.3 29.5 %psum.30 = f32[4]{0:T(128)S(1)} all-reduce(f32[4]{0:T(128)S(1)} %multiply_reduce_fusion), channel_id=1, replica_groups=mesh['pos'=2,'gz'=16] {'gz'}, use_global_device_ids=true, to_apply=%region_6.7 | all-reduce | flops 4 | bytes 32 | tf_op jit(solution)/shard_map/psum | solution.py:80
  108.3 1.8 collective-permute-start.4
  110.2 1.3 collective-permute-start.5
  111.5 11.8 %gather_fusion = s32[2048]{0:T(1024)S(1)} fusion(s32[2048]{0:T(1024)S(1)} %copy-done, s32[2048]{0:T(1024)S(1)} %fusion.41), kind=kCustom, calls=%fused_computation.2 | custom fusion | bytes 24576 | tf_op jit(solution)/shard_map/jit(_take)/gather | solution.py:57
  123.4 3.5 %select_maximum_fusion = f32[4,3,258,258]{3,2,1,0:T(8,128)S(1)} fusion(f32[4,1,256,256]{3,2,1,0:T(8,128)} %collective-permute-done.5, f32[4,1,256,256]{3,2,1,0:T(8,128)S(1)} %multiply_add_fusion.1, f32[4,1,256,256]{3,2,1,0:T(8,128)S(1)} %collective-permute-done.4), kind=kLoop, calls=%fused_computation.7 | loop fusion | flops 11981520 | bytes 6340800 | tf_op jit(solution)/shard_map/concatenate | solution.py:20
  127.0 2.5 %fusion.13 = f32[4]{0:T(128)S(1)} fusion(f32[4,1,256,256]{3,2,1,0:T(8,128)S(1)} %multiply_add_fusion.1, f32[4,3,258,258]{3,2,1,0:T(8,128)S(1)} %select_maximum_fusion, f32[4,1,256,256]{3,2,1,0:T(8,128)} %collective-permute-done.5, f32[4,1,256,256]{3,2,1,0:T(8,128)S(1)} %collective-permute-done.4, f32[256,256]{1,0:T(8,128)S(1)} %copy-done.7, ...), kind=kLoop, calls=%fused_computation.35 | loop fusion | flops 5505020 | bytes 8912912 | tf_op jit(solution)/shard_map/reduce_sum | solution.py:72
  129.5 39.2 %psum.31 = f32[4]{0:T(128)S(1)} all-reduce(f32[4]{0:T(128)S(1)} %fusion.13), channel_id=1, replica_groups=mesh['pos'=2,'gz'=16] {'gz'}, use_global_device_ids=true, to_apply=%region_8.9 | all-reduce | flops 4 | bytes 32 | tf_op jit(solution)/shard_map/psum | solution.py:106
  169.2 1.0 copy-done.3
  170.9 16.5 %copy.33 = f32[4,1,256,256]{0,3,2,1:T(8,128)} copy(f32[4,1,256,256]{3,2,1,0:T(8,128)S(1)} %get-tuple-element.34) | data formatting | bytes 2097152 | tf_op jit(solution)/shard_map/mul | solution.py:55
  187.4 16.0 %gather_fusion.1 = f32[2048,4]{1,0:T(8,128)S(1)} fusion(f32[4,65536]{0,1:T(8,128)} %bitcast.64, s32[2048]{0:T(1024)S(1)} %fusion.42), kind=kCustom, calls=%fused_computation.clone | custom fusion | bytes 73728 | tf_op jit(solution)/shard_map/jit(_take)/gather | solution.py:58
  203.8 16.5 %copy.35 = f32[4,1,256,256]{0,3,2,1:T(8,128)} copy(f32[4,1,256,256]{3,2,1,0:T(8,128)S(1)} %get-tuple-element.33) | data formatting | bytes 2097152 | tf_op jit(solution)/shard_map/mul | solution.py:56
  220.3 16.0 %gather_fusion.2 = f32[2048,4]{1,0:T(8,128)S(1)} fusion(f32[4,65536]{0,1:T(8,128)} %bitcast.63, s32[2048]{0:T(1024)S(1)} %fusion.42), kind=kCustom, calls=%fused_computation.1.clone | custom fusion | bytes 73728 | tf_op jit(solution)/shard_map/jit(_take)/gather | solution.py:59
  237.0 9.1 %all_to_all.4 = f32[8,1,32]{0,1,2:T(1,128)S(1)} all-to-all(f32[8,1,32]{0,1,2:T(1,128)S(1)} %copy.37), channel_id=1, replica_groups=mesh['pos'=2,'gz'=16] {'gz'}, dimensions={2} | all-to-all | bytes 2048 | tf_op jit(solution)/shard_map/all_to_all | solution.py:119
  (67 shorter events, 7.3 us)
Async XLA Ops:
  0.6 110.9 %copy-start = (s32[2048]{0:T(1024)S(1)}, s32[2048]{0:T(1024)}, u32[]{:S(2)}) copy-start(s32[2048]{0:T(1024)} %param.14) | copy-start | bytes 24580
  8.3 14.3 %collective-permute-start.1 = (f32[4,1,256,256]{3,2,1,0:T(8,128)S(1)}, f32[4,1,256,256]{3,2,1,0:T(8,128)S(1)}, u32[]{:S(2)}, u32[]{:S(2)}) collective-permute-start(f32[4,1,256,256]{3,2,1,0:T(8,128)S(1)} %add_multiply_fusion), channel_id=1, source_target_pairs={{0,1},{1,2},{2,3},{3,4},{4,5},{5,6},{6,7},{7,8},{8,9},{9,10},{10,1... | collective-permute-start | bytes 3145736 | tf_op jit(solution)/shard_map/ppermute | solution.py:16
  10.7 11.9 %collective-permute-start.3 = (f32[4,1,256,256]{3,2,1,0:T(8,128)S(1)}, f32[4,1,256,256]{3,2,1,0:T(8,128)S(1)}, u32[]{:S(2)}, u32[]{:S(2)}) collective-permute-start(f32[4,1,256,256]{3,2,1,0:T(8,128)S(1)} %add_multiply_fusion), channel_id=1, source_target_pairs={{1,0},{2,1},{3,2},{4,3},{5,4},{6,5},{7,6},{8,7},{9,8},{10,9},{11,1... | collective-permute-start | bytes 3145736 | tf_op jit(solution)/shard_map/ppermute | solution.py:19
  12.0 6.4 %collective-permute-start = (f32[1,256,256]{2,1,0:T(8,128)S(1)}, f32[1,256,256]{2,1,0:T(8,128)S(1)}, u32[]{:S(2)}, u32[]{:S(2)}) collective-permute-start(f32[1,256,256]{2,1,0:T(8,128)S(1)} %get-tuple-element.24), channel_id=1, source_target_pairs={{0,1},{1,2},{2,3},{3,4},{4,5},{5,6},{6,7},{7,8},{8,9},{9,10},{10,1... | collective-permute-start | bytes 786440 | tf_op jit(solution)/shard_map/ppermute | solution.py:16
  17.2 4.7 %collective-permute-start.2 = (f32[1,256,256]{2,1,0:T(8,128)S(1)}, f32[1,256,256]{2,1,0:T(8,128)S(1)}, u32[]{:S(2)}, u32[]{:S(2)}) collective-permute-start(f32[1,256,256]{2,1,0:T(8,128)S(1)} %get-tuple-element.24), channel_id=1, source_target_pairs={{1,0},{2,1},{3,2},{4,3},{5,4},{6,5},{7,6},{8,7},{9,8},{10,9},{11,1... | collective-permute-start | bytes 786440 | tf_op jit(solution)/shard_map/ppermute | solution.py:19
  22.2 2.8 %copy-start.2 = (f32[1,256,256]{2,1,0:T(8,128)S(1)}, f32[1,256,256]{2,1,0:T(8,128)}, u32[]{:S(2)}) copy-start(f32[1,256,256]{2,1,0:T(8,128)} %param.9) | copy-start | bytes 786436
  22.5 4.3 %copy-start.4 = (f32[256,256]{1,0:T(8,128)}, f32[256,256]{1,0:T(8,128)S(1)}, u32[]{:S(2)}) copy-start(f32[256,256]{1,0:T(8,128)S(1)} %get-tuple-element.29) | copy-start | bytes 786436
  22.5 4.3 %copy-start.6 = (f32[256,256]{1,0:T(8,128)}, f32[256,256]{1,0:T(8,128)S(1)}, u32[]{:S(2)}) copy-start(f32[256,256]{1,0:T(8,128)S(1)} %get-tuple-element.30) | copy-start | bytes 786436
  22.6 4.3 %copy-start.8 = (f32[256,256]{1,0:T(8,128)}, f32[256,256]{1,0:T(8,128)S(1)}, u32[]{:S(2)}) copy-start(f32[256,256]{1,0:T(8,128)S(1)} %get-tuple-element.31) | copy-start | bytes 786436
  22.6 4.3 %copy-start.10 = (f32[256,256]{1,0:T(8,128)}, f32[256,256]{1,0:T(8,128)S(1)}, u32[]{:S(2)}) copy-start(f32[256,256]{1,0:T(8,128)S(1)} %get-tuple-element.32) | copy-start | bytes 786436
  22.6 4.3 %copy-start.12 = (f32[256,256]{1,0:T(8,128)}, f32[256,256]{1,0:T(8,128)S(1)}, u32[]{:S(2)}) copy-start(f32[256,256]{1,0:T(8,128)S(1)} %get-tuple-element.35) | copy-start | bytes 786436
  22.6 4.3 %copy-start.14 = (f32[256,256]{1,0:T(8,128)}, f32[256,256]{1,0:T(8,128)S(1)}, u32[]{:S(2)}) copy-start(f32[256,256]{1,0:T(8,128)S(1)} %get-tuple-element.36) | copy-start | bytes 786436
  26.9 84.6 %copy-start.16 = (s32[2048]{0:T(1024)S(1)}, s32[2048]{0:T(1024)}, u32[]{:S(2)}) copy-start(s32[2048]{0:T(1024)} %param.15) | copy-start | bytes 24580
  108.3 15.1 %collective-permute-start.4 = (f32[4,1,256,256]{3,2,1,0:T(8,128)S(1)}, f32[4,1,256,256]{3,2,1,0:T(8,128)S(1)}, u32[]{:S(2)}, u32[]{:S(2)}) collective-permute-start(f32[4,1,256,256]{3,2,1,0:T(8,128)S(1)} %multiply_add_fusion.1), channel_id=1, source_target_pairs={{0,1},{1,2},{2,3},{3,4},{4,5},{5,6},{6,7},{7,8},{8,9},{9,10},{10,1... | collective-permute-start | bytes 3145736 | tf_op jit(solution)/shard_map/ppermute | solution.py:16
  110.2 13.3 %collective-permute-start.5 = (f32[4,1,256,256]{3,2,1,0:T(8,128)S(1)}, f32[4,1,256,256]{3,2,1,0:T(8,128)}, u32[]{:S(2)}, u32[]{:S(2)}) collective-permute-start(f32[4,1,256,256]{3,2,1,0:T(8,128)S(1)} %multiply_add_fusion.1), channel_id=1, source_target_pairs={{1,0},{2,1},{3,2},{4,3},{5,4},{6,5},{7,6},{8,7},{9,8},{10,9},{11,1... | collective-permute-start | bytes 3145736 | tf_op jit(solution)/shard_map/ppermute | solution.py:19
  123.3 3.7 %copy-start.5 = (f32[256,256]{1,0:T(8,128)S(1)}, f32[256,256]{1,0:T(8,128)}, u32[]{:S(2)}) copy-start(f32[256,256]{1,0:T(8,128)} %copy-done.4) | copy-start | bytes 786436
  123.3 3.7 %copy-start.7 = (f32[256,256]{1,0:T(8,128)S(1)}, f32[256,256]{1,0:T(8,128)}, u32[]{:S(2)}) copy-start(f32[256,256]{1,0:T(8,128)} %copy-done.6) | copy-start | bytes 786436
  123.3 3.7 %copy-start.9 = (f32[256,256]{1,0:T(8,128)S(1)}, f32[256,256]{1,0:T(8,128)}, u32[]{:S(2)}) copy-start(f32[256,256]{1,0:T(8,128)} %copy-done.8) | copy-start | bytes 786436
  123.3 3.7 %copy-start.11 = (f32[256,256]{1,0:T(8,128)S(1)}, f32[256,256]{1,0:T(8,128)}, u32[]{:S(2)}) copy-start(f32[256,256]{1,0:T(8,128)} %copy-done.10) | copy-start | bytes 786436
  123.3 3.7 %copy-start.13 = (f32[256,256]{1,0:T(8,128)S(1)}, f32[256,256]{1,0:T(8,128)}, u32[]{:S(2)}) copy-start(f32[256,256]{1,0:T(8,128)} %copy-done.12) | copy-start | bytes 786436
  123.3 3.7 %copy-start.15 = (f32[256,256]{1,0:T(8,128)S(1)}, f32[256,256]{1,0:T(8,128)}, u32[]{:S(2)}) copy-start(f32[256,256]{1,0:T(8,128)} %copy-done.14) | copy-start | bytes 786436
  169.2 1.0 copy-start.3
  203.8 44.3 %copy-start.1 = (s32[2048]{0:T(1024)S(1)}, s32[2048]{0:T(1024)}, u32[]{:S(2)}) copy-start(s32[2048]{0:T(1024)} %param.14) | copy-start | bytes 24580
where the time goes:
time: 249 us; the launch traced here: 248 us
  blocking collectives  129 us (52%)
  local copies, waits for them, and re-layouts  81.7 us (33%)
  other arithmetic  20.1 us (8%)
  starting transfers between devices  13.2 us (5%)
  waiting for transfers between devices  3.36 us (1%)
    psum x2, blocking collectives, squares(): return lax.psum(column_sum(residual, residual), 'gz')  80.3 us
    psum x1, blocking collectives, body(): curvature = lax.psum(column_sum(direction, image), 'gz')  39.2 us
    mul x1, local copies, waits for them, and re-layouts, band_stress(): flux_x = 0.5 * (padded[:, :, 1:-1, 2:] - padded[:, :, 1:-1, :-2])  16.5 us
    mul x1, local copies, waits for them, and re-layouts, band_stress(): flux_y = -0.5 * (padded[:, :, 2:, 1:-1] - padded[:, :, :-2, 1:-1])  16.5 us
    gather x2, local copies, waits for them, and re-layouts, band_stress(): jnp.take(flux_x.reshape(count_cols, depth, width_x * width_y), ordered, a...  16.3 us
    gather x2, local copies, waits for them, and re-layouts, band_stress(): jnp.take(flux_y.reshape(count_cols, depth, width_x * width_y), ordered, a...  16.3 us
    gather x1, local copies, waits for them, and re-layouts, band_stress(): ordered = jnp.take(band_cells, sector_order)  11.8 us
    ppermute x3, starting transfers between devices, with_halo(): lax.ppermute(lax.slice_in_dim(block, block.shape[dim] - width, None, axis...  9.37 us
  transfers between devices with their start and end apart: 6, of which 1 were waited for; matrix products, arithmetic and copies ran while one was open for 5% of the time, Pallas kernels for 0%

commit v1 on v0

--- a/solution.py
+++ b/solution.py
@@ -6,6 +6,29 @@
 ITERS = 2
 PER_SEC = 64
 MASS_SHIFT = 0.5
+
+
+def cut_along(x, dim, size):
+    lengths = x.shape
+    tiles = x.reshape(*lengths[:dim], size, lengths[dim] // size, *lengths[dim + 1 :])
+    return jnp.moveaxis(tiles, dim, 0)
+
+
+def in_order(blocks, dim):
+    dims = list(blocks.shape[1:])
+    dims[dim] *= blocks.shape[0]
+    return jnp.moveaxis(blocks, 0, dim).reshape(dims)
+
+
+def exchange_in_pairs(shard, axis, split_dim, concat_dim):
+    devices, position = (lax.axis_size(axis), lax.axis_index(axis))
+    blocks = cut_along(shard, split_dim, devices)
+    finished = [blocks[position]]
+    for lap in range(1, devices):
+        sent = blocks[position ^ lap]
+        finished.append(lax.ppermute(sent, axis, [(i, i ^ lap) for i in range(devices)]))
+    blocks = jnp.stack(finished)[position ^ jnp.arange(devices)]
+    return in_order(blocks, concat_dim)
 
 
 def with_halo(block, sides, width):
@@ -116,7 +139,7 @@
     band_total = stress.shape[3]
     cell_forces = stress.reshape(2 * count_cols, depth, band_total // PER_SEC, PER_SEC)
     sector_sums = jnp.sum(cell_forces, axis=-1)
-    gathered = lax.all_to_all(sector_sums, "gz", split_axis=2, concat_axis=1, tiled=True)
+    gathered = exchange_in_pairs(sector_sums, "gz", 2, 1)
     full_depth = gathered.shape[1]
     local_sectors = gathered.shape[2]
     return (

time: 249 us -> 267 us (1.072)
  starting transfers between devices: 13.2 us -> 34.4 us
  blocking collectives: 129 us -> 120 us
  other arithmetic: 20.1 us -> 25.8 us
    ppermute x0 -> x15, starting transfers between devices: none -> 20.5 us  [exchange_in_pairs(): lax.ppermute(sent, axis, [(i, i ^ lap) for i in range(devices)])]
    all_to_all x1 -> x0, blocking collectives: 9.06 us -> none  [body(): lax.all_to_all(sector_sums, 'gz', split_axis=2, concat_axis=1, tiled=True)]
  transfers between devices with their start and end apart: 6 -> 21, of which waited for: 1 -> 2; matrix products, arithmetic and copies ran while one was open for 5% -> 6% of each run, Pallas kernels for 0% -> 0%
where the time goes in v1:
time: 267 us; the launch traced here: 266 us
  blocking collectives  120 us (45%)
  local copies, waits for them, and re-layouts  81.1 us (30%)
  starting transfers between devices  34.4 us (13%)
  other arithmetic  25.8 us (10%)
  waiting for transfers between devices  3.84 us (1%)
    psum x2, blocking collectives, squares(): return lax.psum(column_sum(residual, residual), 'gz')  80.5 us
    psum x1, blocking collectives, body(): curvature = lax.psum(column_sum(direction, image), 'gz')  39 us
    ppermute x15, starting transfers between devices, exchange_in_pairs(): lax.ppermute(sent, axis, [(i, i ^ lap) for i in range(devices)])  20.5 us
    mul x1, local copies, waits for them, and re-layouts, band_stress(): flux_x = 0.5 * (padded[:, :, 1:-1, 2:] - padded[:, :, 1:-1, :-2])  16.6 us
    mul x1, local copies, waits for them, and re-layouts, band_stress(): flux_y = -0.5 * (padded[:, :, 2:, 1:-1] - padded[:, :, :-2, 1:-1])  16.6 us
    gather x2, local copies, waits for them, and re-layouts, band_stress(): jnp.take(flux_x.reshape(count_cols, depth, width_x * width_y), ordered, a...  16.3 us
    gather x2, local copies, waits for them, and re-layouts, band_stress(): jnp.take(flux_y.reshape(count_cols, depth, width_x * width_y), ordered, a...  16.3 us
    gather x1, local copies, waits for them, and re-layouts, band_stress(): ordered = jnp.take(band_cells, sector_order)  11.8 us
  transfers between devices with their start and end apart: 21, of which 2 were waited for; matrix products, arithmetic and copies ran while one was open for 6% of the time, Pallas kernels for 0%

profile of v1, /device:TPU:0, one launch (start us, length us, event | category | flops | bytes accessed | tf_op | source)
XLA Modules:
  0.0 266.0 jit_solution(5032191866792451002)
XLA Ops:
  3.2 3.7 %select_add_fusion = (f32[1,256,256]{2,1,0:T(8,128)S(1)}, pred[1,256,256]{2,1,0:T(8,128)(4,1)S(1)}, pred[1,256,256]{2,1,0:T(8,128)(4,1)S(1)}, pred[1,256,256]{2,1,0:T(8,128)(4,1)S(1)}, pred[1,256,256]{2,1,0:T(8,128)(4,1)S(1)}) fusion(f32[]{:T(128)} %bitcast.8, f32[]{:T(128)} %bitcast.7, f32[]{:T(128)} %bitcast.6, f32[]{:T(128)} %bitcast.5, ...), kind=kLoop, calls=%fused_computation.83 | loop fusion | flops 720896 | bytes 786448 | tf_op jit(solution)/shard_map/add | solution.py:118
  7.0 2.3 add_multiply_fusion
  9.3 2.4 collective-permute-start.1
  13.0 5.8 %collective-permute-start = (f32[1,256,256]{2,1,0:T(8,128)S(1)}, f32[1,256,256]{2,1,0:T(8,128)}, u32[]{:S(2)}, u32[]{:S(2)}) collective-permute-start(f32[1,256,256]{2,1,0:T(8,128)S(1)} %get-tuple-element.26), channel_id=1, source_target_pairs={{0,1},{1,2},{2,3},{3,4},{4,5},{5,6},{6,7},{7,8},{8,9},{9,10},{10,1... | collective-permute-start | bytes 786440 | tf_op jit(solution)/shard_map/ppermute | solution.py:39
  20.8 2.1 collective-permute-done.2
  25.9 3.8 %select_maximum_fusion.2 = f32[4,3,258,258]{3,2,1,0:T(8,128)S(1)} fusion(f32[4,1,256,256]{3,2,1,0:T(8,128)S(1)} %collective-permute-done.3, f32[4,1,256,256]{3,2,1,0:T(8,128)} %add_multiply_fusion, f32[4,1,256,256]{3,2,1,0:T(8,128)S(1)} %collective-permute-done.1), kind=kLoop, calls=%fused_computation.10 | loop fusion | flops 11981520 | bytes 6340800 | tf_op jit(solution)/shard_map/concatenate | solution.py:43
  29.7 3.0 %multiply_reduce_fusion.1 = (f32[4]{0:T(128)S(1)}, f32[4]{0:T(128)S(1)}, f32[4,1,256,256]{3,2,1,0:T(8,128)S(1)}) fusion(f32[4,3,258,258]{3,2,1,0:T(8,128)S(1)} %select_maximum_fusion.2, f32[256,256]{1,0:T(8,128)S(1)} %get-tuple-element.32, f32[256,256]{1,0:T(8,128)S(1)} %get-tuple-element.33, f32[256,256]{1,0:T(8,128)S(1)} %get-tuple-element.34, ...), kind=kLoop, calls=%fused_computation.62 | loop fusion | flops 8126456 | bytes 10223712 | tf_op jit(solution)/shard_map/reduce_sum | solution.py:95
  32.7 51.0 %all-reduce.4 = (f32[4]{0:T(128)S(1)}, f32[4]{0:T(128)S(1)}) all-reduce(f32[4]{0:T(128)S(1)} %get-tuple-element.16, f32[4]{0:T(128)S(1)} %get-tuple-element.15), channel_id=1, replica_groups=mesh['pos'=2,'gz'=16] {'gz'}, use_global_device_ids=true, to_apply=%region_2.3 | all-reduce | flops 8 | bytes 64 | tf_op jit(solution)/shard_map/psum | solution.py:103
  84.4 29.5 %psum.30 = f32[4]{0:T(128)S(1)} all-reduce(f32[4]{0:T(128)S(1)} %multiply_reduce_fusion), channel_id=1, replica_groups=mesh['pos'=2,'gz'=16] {'gz'}, use_global_device_ids=true, to_apply=%region_6.7 | all-reduce | flops 4 | bytes 32 | tf_op jit(solution)/shard_map/psum | solution.py:103
  114.3 1.8 collective-permute-start.4
  117.6 11.8 %gather_fusion = s32[2048]{0:T(1024)S(1)} fusion(s32[2048]{0:T(1024)S(1)} %copy-done, s32[2048]{0:T(1024)S(1)} %fusion.41), kind=kCustom, calls=%fused_computation.2 | custom fusion | bytes 24576 | tf_op jit(solution)/shard_map/jit(_take)/gather | solution.py:80
  129.6 3.5 %select_maximum_fusion = f32[4,3,258,258]{3,2,1,0:T(8,128)S(1)} fusion(f32[4,1,256,256]{3,2,1,0:T(8,128)} %collective-permute-done.5, f32[4,1,256,256]{3,2,1,0:T(8,128)S(1)} %multiply_add_fusion.1, f32[4,1,256,256]{3,2,1,0:T(8,128)S(1)} %collective-permute-done.4), kind=kLoop, calls=%fused_computation.8 | loop fusion | flops 11981520 | bytes 6340800 | tf_op jit(solution)/shard_map/concatenate | solution.py:43
  133.2 2.5 fusion.13
  135.7 39.0 %psum.31 = f32[4]{0:T(128)S(1)} all-reduce(f32[4]{0:T(128)S(1)} %fusion.13), channel_id=1, replica_groups=mesh['pos'=2,'gz'=16] {'gz'}, use_global_device_ids=true, to_apply=%region_8.9 | all-reduce | flops 4 | bytes 32 | tf_op jit(solution)/shard_map/psum | solution.py:129
  176.0 16.6 %copy.60 = f32[4,1,256,256]{0,3,2,1:T(8,128)} copy(f32[4,1,256,256]{3,2,1,0:T(8,128)S(1)} %get-tuple-element.36) | data formatting | bytes 2097152 | tf_op jit(solution)/shard_map/mul | solution.py:78
  192.6 16.0 %gather_fusion.2 = f32[2048,4]{1,0:T(8,128)S(1)} fusion(f32[4,65536]{0,1:T(8,128)} %bitcast.134, s32[2048]{0:T(1024)S(1)} %fusion.42), kind=kCustom, calls=%fused_computation.clone | custom fusion | bytes 73728 | tf_op jit(solution)/shard_map/jit(_take)/gather | solution.py:81
  208.9 16.6 %copy.62 = f32[4,1,256,256]{0,3,2,1:T(8,128)} copy(f32[4,1,256,256]{3,2,1,0:T(8,128)S(1)} %get-tuple-element.35) | data formatting | bytes 2097152 | tf_op jit(solution)/shard_map/mul | solution.py:79
  225.5 16.0 %gather_fusion.3 = f32[2048,4]{1,0:T(8,128)S(1)} fusion(f32[4,65536]{0,1:T(8,128)} %bitcast.133, s32[2048]{0:T(1024)S(1)} %fusion.42), kind=kCustom, calls=%fused_computation.1.clone | custom fusion | bytes 73728 | tf_op jit(solution)/shard_map/jit(_take)/gather | solution.py:82
  242.5 1.8 collective-permute-start.8
  246.0 2.6 collective-permute-start.12
  248.7 2.6 collective-permute-start.14
  251.4 3.5 %collective-permute-start.16 = (f32[8,1,2]{0,2,1:T(2,128)S(1)}, f32[8,1,2]{0,2,1:T(2,128)S(1)}, u32[]{:S(2)}, u32[]{:S(2)}) collective-permute-start(f32[8,1,2]{0,2,1:T(2,128)S(1)} %get-tuple-element.45), channel_id=1, source_target_pairs={{0,11},{1,10},{2,9},{3,8},{4,15},{5,14},{6,13},{7,12},{8,3},{9,2},... | collective-permute-start | bytes 200 | tf_op jit(solution)/shard_map/ppermute | solution.py:29
  255.0 3.5 %collective-permute-start.18 = (f32[8,1,2]{0,2,1:T(2,128)S(1)}, f32[8,1,2]{0,2,1:T(2,128)S(1)}, u32[]{:S(2)}, u32[]{:S(2)}) collective-permute-start(f32[8,1,2]{0,2,1:T(2,128)S(1)} %get-tuple-element.43), channel_id=1, source_target_pairs={{0,13},{1,12},{2,15},{3,14},{4,9},{5,8},{6,11},{7,10},{8,5},{9,4},... | collective-permute-start | bytes 200 | tf_op jit(solution)/shard_map/ppermute | solution.py:29
  258.7 4.3 %collective-permute-start.20 = (f32[8,1,2]{0,2,1:T(2,128)S(1)}, f32[8,1,2]{0,2,1:T(2,128)S(1)}, u32[]{:S(2)}, u32[]{:S(2)}) collective-permute-start(f32[8,1,2]{0,2,1:T(2,128)S(1)} %get-tuple-element.41), channel_id=1, source_target_pairs={{0,15},{1,14},{2,13},{3,12},{4,11},{5,10},{6,9},{7,8},{8,7},{9,6},... | collective-permute-start | bytes 200 | tf_op jit(solution)/shard_map/ppermute | solution.py:29
  (118 shorter events, 18.9 us)
Async XLA Ops:
  0.6 116.9 %copy-start = (s32[2048]{0:T(1024)S(1)}, s32[2048]{0:T(1024)}, u32[]{:S(2)}) copy-start(s32[2048]{0:T(1024)} %param.14) | copy-start | bytes 24580
  9.3 16.6 %collective-permute-start.1 = (f32[4,1,256,256]{3,2,1,0:T(8,128)}, f32[4,1,256,256]{3,2,1,0:T(8,128)S(1)}, u32[]{:S(2)}, u32[]{:S(2)}) collective-permute-start(f32[4,1,256,256]{3,2,1,0:T(8,128)} %add_multiply_fusion), channel_id=1, source_target_pairs={{0,1},{1,2},{2,3},{3,4},{4,5},{5,6},{6,7},{7,8},{8,9},{9,10},{10,1... | collective-permute-start | bytes 3145736 | tf_op jit(solution)/shard_map/ppermute | solution.py:39
  11.7 14.2 %collective-permute-start.3 = (f32[4,1,256,256]{3,2,1,0:T(8,128)}, f32[4,1,256,256]{3,2,1,0:T(8,128)S(1)}, u32[]{:S(2)}, u32[]{:S(2)}) collective-permute-start(f32[4,1,256,256]{3,2,1,0:T(8,128)} %add_multiply_fusion), channel_id=1, source_target_pairs={{1,0},{2,1},{3,2},{4,3},{5,4},{6,5},{7,6},{8,7},{9,8},{10,9},{11,1... | collective-permute-start | bytes 3145736 | tf_op jit(solution)/shard_map/ppermute | solution.py:42
  13.0 7.8 %collective-permute-start = (f32[1,256,256]{2,1,0:T(8,128)S(1)}, f32[1,256,256]{2,1,0:T(8,128)}, u32[]{:S(2)}, u32[]{:S(2)}) collective-permute-start(f32[1,256,256]{2,1,0:T(8,128)S(1)} %get-tuple-element.26), channel_id=1, source_target_pairs={{0,1},{1,2},{2,3},{3,4},{4,5},{5,6},{6,7},{7,8},{8,9},{9,10},{10,1... | collective-permute-start | bytes 786440 | tf_op jit(solution)/shard_map/ppermute | solution.py:39
  18.8 4.1 %collective-permute-start.2 = (f32[1,256,256]{2,1,0:T(8,128)S(1)}, f32[1,256,256]{2,1,0:T(8,128)}, u32[]{:S(2)}, u32[]{:S(2)}) collective-permute-start(f32[1,256,256]{2,1,0:T(8,128)S(1)} %get-tuple-element.26), channel_id=1, source_target_pairs={{1,0},{2,1},{3,2},{4,3},{5,4},{6,5},{7,6},{8,7},{9,8},{10,9},{11,1... | collective-permute-start | bytes 786440 | tf_op jit(solution)/shard_map/ppermute | solution.py:42
  114.3 15.3 %collective-permute-start.4 = (f32[4,1,256,256]{3,2,1,0:T(8,128)S(1)}, f32[4,1,256,256]{3,2,1,0:T(8,128)S(1)}, u32[]{:S(2)}, u32[]{:S(2)}) collective-permute-start(f32[4,1,256,256]{3,2,1,0:T(8,128)S(1)} %multiply_add_fusion.1), channel_id=1, source_target_pairs={{0,1},{1,2},{2,3},{3,4},{4,5},{5,6},{6,7},{7,8},{8,9},{9,10},{10,1... | collective-permute-start | bytes 3145736 | tf_op jit(solution)/shard_map/ppermute | solution.py:39
  116.2 13.4 %collective-permute-start.5 = (f32[4,1,256,256]{3,2,1,0:T(8,128)S(1)}, f32[4,1,256,256]{3,2,1,0:T(8,128)}, u32[]{:S(2)}, u32[]{:S(2)}) collective-permute-start(f32[4,1,256,256]{3,2,1,0:T(8,128)S(1)} %multiply_add_fusion.1), channel_id=1, source_target_pairs={{1,0},{2,1},{3,2},{4,3},{5,4},{6,5},{7,6},{8,7},{9,8},{10,9},{11,1... | collective-permute-start | bytes 3145736 | tf_op jit(solution)/shard_map/ppermute | solution.py:42
  175.2 17.4 %copy-start.4 = (f32[4,1,256,256]{3,2,1,0:T(8,128)}, f32[4,1,256,256]{3,2,1,0:T(8,128)S(1)}, u32[]{:S(2)}) copy-start(f32[4,1,256,256]{3,2,1,0:T(8,128)S(1)} %multiply_add_fusion) | copy-start | bytes 3145732
  208.9 57.1 %copy-start.1 = (s32[2048]{0:T(1024)S(1)}, s32[2048]{0:T(1024)}, u32[]{:S(2)}) copy-start(s32[2048]{0:T(1024)} %param.14) | copy-start | bytes 24580
  242.3 3.7 %collective-permute-start.6 = (f32[8,1,2]{0,2,1:T(2,128)S(1)}, f32[8,1,2]{0,2,1:T(2,128)S(1)}, u32[]{:S(2)}, u32[]{:S(2)}) collective-permute-start(f32[8,1,2]{0,2,1:T(2,128)S(1)} %get-tuple-element.55), channel_id=1, source_target_pairs={{0,1},{1,0},{2,3},{3,2},{4,5},{5,4},{6,7},{7,6},{8,9},{9,8},{10,11... | collective-permute-start | bytes 200 | tf_op jit(solution)/shard_map/ppermute | solution.py:29
  242.4 3.6 %collective-permute-start.7 = (f32[8,1,2]{0,2,1:T(2,128)S(1)}, f32[8,1,2]{0,2,1:T(2,128)S(1)}, u32[]{:S(2)}, u32[]{:S(2)}) collective-permute-start(f32[8,1,2]{0,2,1:T(2,128)S(1)} %get-tuple-element.54), channel_id=1, source_target_pairs={{0,2},{1,3},{2,0},{3,1},{4,6},{5,7},{6,4},{7,5},{8,10},{9,11},{10,... | collective-permute-start | bytes 200 | tf_op jit(solution)/shard_map/ppermute | solution.py:29
  242.5 6.2 %collective-permute-start.8 = (f32[8,1,2]{0,2,1:T(2,128)S(1)}, f32[8,1,2]{0,2,1:T(2,128)S(1)}, u32[]{:S(2)}, u32[]{:S(2)}) collective-permute-start(f32[8,1,2]{0,2,1:T(2,128)S(1)} %get-tuple-element.53), channel_id=1, source_target_pairs={{0,3},{1,2},{2,1},{3,0},{4,7},{5,6},{6,5},{7,4},{8,11},{9,10},{10,... | collective-permute-start | bytes 200 | tf_op jit(solution)/shard_map/ppermute | solution.py:29
  244.3 4.5 %collective-permute-start.9 = (f32[8,1,2]{0,2,1:T(2,128)S(1)}, f32[8,1,2]{0,2,1:T(2,128)S(1)}, u32[]{:S(2)}, u32[]{:S(2)}) collective-permute-start(f32[8,1,2]{0,2,1:T(2,128)S(1)} %get-tuple-element.52), channel_id=1, source_target_pairs={{0,4},{1,5},{2,6},{3,7},{4,0},{5,1},{6,2},{7,3},{8,12},{9,13},{10,... | collective-permute-start | bytes 200 | tf_op jit(solution)/shard_map/ppermute | solution.py:29
  244.3 7.0 %collective-permute-start.10 = (f32[8,1,2]{0,2,1:T(2,128)S(1)}, f32[8,1,2]{0,2,1:T(2,128)S(1)}, u32[]{:S(2)}, u32[]{:S(2)}) collective-permute-start(f32[8,1,2]{0,2,1:T(2,128)S(1)} %get-tuple-element.51), channel_id=1, source_target_pairs={{0,5},{1,4},{2,7},{3,6},{4,1},{5,0},{6,3},{7,2},{8,13},{9,12},{10,... | collective-permute-start | bytes 200 | tf_op jit(solution)/shard_map/ppermute | solution.py:29
  246.0 5.5 %collective-permute-start.11 = (f32[8,1,2]{0,2,1:T(2,128)S(1)}, f32[8,1,2]{0,2,1:T(2,128)S(1)}, u32[]{:S(2)}, u32[]{:S(2)}) collective-permute-start(f32[8,1,2]{0,2,1:T(2,128)S(1)} %get-tuple-element.50), channel_id=1, source_target_pairs={{0,6},{1,7},{2,4},{3,5},{4,2},{5,3},{6,0},{7,1},{8,14},{9,15},{10,... | collective-permute-start | bytes 200 | tf_op jit(solution)/shard_map/ppermute | solution.py:29
  246.0 8.9 %collective-permute-start.12 = (f32[8,1,2]{0,2,1:T(2,128)S(1)}, f32[8,1,2]{0,2,1:T(2,128)S(1)}, u32[]{:S(2)}, u32[]{:S(2)}) collective-permute-start(f32[8,1,2]{0,2,1:T(2,128)S(1)} %get-tuple-element.49), channel_id=1, source_target_pairs={{0,7},{1,6},{2,5},{3,4},{4,3},{5,2},{6,1},{7,0},{8,15},{9,14},{10,... | collective-permute-start | bytes 200 | tf_op jit(solution)/shard_map/ppermute | solution.py:29
  248.7 6.3 %collective-permute-start.13 = (f32[8,1,2]{0,2,1:T(2,128)S(1)}, f32[8,1,2]{0,2,1:T(2,128)S(1)}, u32[]{:S(2)}, u32[]{:S(2)}) collective-permute-start(f32[8,1,2]{0,2,1:T(2,128)S(1)} %get-tuple-element.48), channel_id=1, source_target_pairs={{0,8},{1,9},{2,10},{3,11},{4,12},{5,13},{6,14},{7,15},{8,0},{9,1},... | collective-permute-start | bytes 200 | tf_op jit(solution)/shard_map/ppermute | solution.py:29
  248.7 9.7 %collective-permute-start.14 = (f32[8,1,2]{0,2,1:T(2,128)S(1)}, f32[8,1,2]{0,2,1:T(2,128)S(1)}, u32[]{:S(2)}, u32[]{:S(2)}) collective-permute-start(f32[8,1,2]{0,2,1:T(2,128)S(1)} %get-tuple-element.47), channel_id=1, source_target_pairs={{0,9},{1,8},{2,11},{3,10},{4,13},{5,12},{6,15},{7,14},{8,1},{9,0},... | collective-permute-start | bytes 200 | tf_op jit(solution)/shard_map/ppermute | solution.py:29
  251.3 7.3 %collective-permute-start.15 = (f32[8,1,2]{0,2,1:T(2,128)S(1)}, f32[8,1,2]{0,2,1:T(2,128)S(1)}, u32[]{:S(2)}, u32[]{:S(2)}) collective-permute-start(f32[8,1,2]{0,2,1:T(2,128)S(1)} %get-tuple-element.46), channel_id=1, source_target_pairs={{0,10},{1,11},{2,8},{3,9},{4,14},{5,15},{6,12},{7,13},{8,2},{9,3},... | collective-permute-start | bytes 200 | tf_op jit(solution)/shard_map/ppermute | solution.py:29
  251.4 11.5 %collective-permute-start.16 = (f32[8,1,2]{0,2,1:T(2,128)S(1)}, f32[8,1,2]{0,2,1:T(2,128)S(1)}, u32[]{:S(2)}, u32[]{:S(2)}) collective-permute-start(f32[8,1,2]{0,2,1:T(2,128)S(1)} %get-tuple-element.45), channel_id=1, source_target_pairs={{0,11},{1,10},{2,9},{3,8},{4,15},{5,14},{6,13},{7,12},{8,3},{9,2},... | collective-permute-start | bytes 200 | tf_op jit(solution)/shard_map/ppermute | solution.py:29
  254.9 8.0 %collective-permute-start.17 = (f32[8,1,2]{0,2,1:T(2,128)S(1)}, f32[8,1,2]{0,2,1:T(2,128)S(1)}, u32[]{:S(2)}, u32[]{:S(2)}) collective-permute-start(f32[8,1,2]{0,2,1:T(2,128)S(1)} %get-tuple-element.44), channel_id=1, source_target_pairs={{0,12},{1,13},{2,14},{3,15},{4,8},{5,9},{6,10},{7,11},{8,4},{9,5},... | collective-permute-start | bytes 200 | tf_op jit(solution)/shard_map/ppermute | solution.py:29
  255.0 8.0 %collective-permute-start.18 = (f32[8,1,2]{0,2,1:T(2,128)S(1)}, f32[8,1,2]{0,2,1:T(2,128)S(1)}, u32[]{:S(2)}, u32[]{:S(2)}) collective-permute-start(f32[8,1,2]{0,2,1:T(2,128)S(1)} %get-tuple-element.43), channel_id=1, source_target_pairs={{0,13},{1,12},{2,15},{3,14},{4,9},{5,8},{6,11},{7,10},{8,5},{9,4},... | collective-permute-start | bytes 200 | tf_op jit(solution)/shard_map/ppermute | solution.py:29
  258.4 6.3 %collective-permute-start.19 = (f32[8,1,2]{0,2,1:T(2,128)S(1)}, f32[8,1,2]{0,2,1:T(2,128)S(1)}, u32[]{:S(2)}, u32[]{:S(2)}) collective-permute-start(f32[8,1,2]{0,2,1:T(2,128)S(1)} %get-tuple-element.42), channel_id=1, source_target_pairs={{0,14},{1,15},{2,12},{3,13},{4,10},{5,11},{6,8},{7,9},{8,6},{9,7},... | collective-permute-start | bytes 200 | tf_op jit(solution)/shard_map/ppermute | solution.py:29
  258.7 6.1 %collective-permute-start.20 = (f32[8,1,2]{0,2,1:T(2,128)S(1)}, f32[8,1,2]{0,2,1:T(2,128)S(1)}, u32[]{:S(2)}, u32[]{:S(2)}) collective-permute-start(f32[8,1,2]{0,2,1:T(2,128)S(1)} %get-tuple-element.41), channel_id=1, source_target_pairs={{0,15},{1,14},{2,13},{3,12},{4,11},{5,10},{6,9},{7,8},{8,7},{9,6},... | collective-permute-start | bytes 200 | tf_op jit(solution)/shard_map/ppermute | solution.py:29
  (16 other events, 103.9 us)
